TPU v7x, 32 devices: a whole 2x2x4 slice. The times are simulated.
32 devices in a mesh: seq: 16 (over z, x, core), head: 2 (over y).
Axes of the slice: x: 2, y: 2, z: 4, core: 2. Of those that a mesh axis runs over, the one named last changes fastest.
Arguments:
- features: bfloat16 [8, 32, 8, 512], P(None, 'seq', 'head'), may hold values from -540 to 540
- gn_gain: float32 [512], replicated, may hold values from 0.5 to 1.5
- gn_bias: float32 [512], replicated, may hold values from -3 to 3
- conv_weight: bfloat16 [3, 3, 3, 16, 512], replicated, may hold values from -0.0546875 to 0.0546875
- conv_bias: float32 [16], replicated, may hold values from -3 to 3
- patch_weight: bfloat16 [64, 3072], replicated, may hold values from -0.75 to 0.75
- patch_bias: float32 [3072], replicated, may hold values from -3 to 3
- image_mod: float32 [3, 3072], replicated, may hold values from -3 to 3
- w_qkv: bfloat16 [3072, 3, 2048], P('seq', None, 'head'), may hold values from -5 to 5
- text_ids: int32 [512], replicated, may hold values from 0 to 16383
- text_length: int32 [1], replicated, may hold values from 256 to 512
- text_table: bfloat16 [3072, 16384], P('seq'), may hold values from -60 to 60
- text_mod: float32 [2, 3072], P(None, 'seq'), may hold values from -3 to 3
- w_text: bfloat16 [3072, 2, 2048], P('seq', None, 'head'), may hold values from -2 to 2
- w_out: bfloat16 [2048, 3072], P('head'), may hold values from -0.625 to 0.625
- out_bias: float32 [3072], replicated, may hold values from -3 to 3
Outputs:
- block_out: bfloat16 [8, 16, 4, 3072], P(None, 'seq', 'head')
All inputs are finite; a program needn't handle non-finite values.
Results may differ from a plain program's by a relative error of at most 0.0089.
Values may be sent and summed in bfloat16 or wider, within the bound.
A program may use at most 128 MiB of HBM per device.

v0:
```python
import math
import jax
import jax.numpy as jnp
from jax import lax
from jax.sharding import PartitionSpec as P

HD = 128
GN_GROUPS = 32
eps_norm = 1e-06


def with_halo(cells, sides, width):
    for axis, dim in sides:
        count = lax.axis_size(axis)
        ends = count - 1
        head = lax.slice_in_dim(cells, 0, width, axis=dim)
        tail = lax.slice_in_dim(cells, cells.shape[dim] - width, cells.shape[dim], axis=dim)
        cells = jnp.concatenate(
            [
                lax.ppermute(tail, axis, [(i, (i + 1) % count) for i in range(ends)]),
                cells,
                lax.ppermute(head, axis, [((i + 1) % count, i) for i in range(ends)]),
            ],
            axis=dim,
        )
    return cells


def patchify(latent):
    frame_count, row_count, col_count, chan_count = latent.shape
    blocks = latent.reshape(frame_count, row_count // 2, 2, col_count // 2, 2, chan_count)
    blocks = blocks.transpose(0, 1, 3, 2, 4, 5)
    return blocks.reshape(frame_count * (row_count // 2) * (col_count // 2), 4 * chan_count)


def embed_tokens(patches, patch_weight, patch_bias, image_mod):
    hidden = jnp.dot(patches, patch_weight, preferred_element_type=jnp.float32) + patch_bias
    center = jnp.mean(hidden, axis=1, keepdims=True)
    offset = hidden - center
    spread = jnp.mean(offset * offset, axis=1, keepdims=True)
    normed = offset * lax.rsqrt(spread + eps_norm)
    modulated = (normed * (1.0 + image_mod[1]) + image_mod[0]).astype(jnp.bfloat16)
    return (hidden, modulated)


def text_start(query, text_keys, text_values, text_valid):
    scores = jnp.einsum("qhe,khe->qhk", query, text_keys, preferred_element_type=jnp.float32) / HD
    scores = jnp.where(text_valid[None, None, :], scores, -1e30)
    first_top = jnp.max(scores, axis=2)
    probs = jnp.exp(scores - first_top[..., None])
    first_total = jnp.sum(probs, axis=2)
    first_acc = jnp.einsum(
        "qhk,khe->qhe", probs.astype(jnp.bfloat16), text_values, preferred_element_type=jnp.float32
    )
    return (first_top, first_total, first_acc)


def attend_rows(query, state, piece):
    piece_rows = piece.shape[0]
    block_rows = math.gcd(piece_rows, 2048)
    heads_count = query.shape[1]
    blocks = piece.reshape(piece_rows // block_rows, block_rows, 2, heads_count, HD)

    def one_block(inner, block):
        run_top, run_total, run_acc = inner
        scores = (
            jnp.einsum("qhe,khe->qhk", query, block[:, 0], preferred_element_type=jnp.float32) / HD
        )
        new_top = jnp.maximum(run_top, jnp.max(scores, axis=2))
        factor = jnp.exp(run_top - new_top)
        probs = jnp.exp(scores - new_top[..., None])
        run_total = run_total * factor + jnp.sum(probs, axis=2)
        run_acc = run_acc * factor[..., None] + jnp.einsum(
            "qhk,khe->qhe",
            probs.astype(jnp.bfloat16),
            block[:, 1],
            preferred_element_type=jnp.float32,
        )
        return ((new_top, run_total, run_acc), None)

    return lax.scan(one_block, state, blocks)[0]


def body(
    features,
    gn_gain,
    gn_bias,
    conv_weight,
    conv_bias,
    patch_weight,
    patch_bias,
    image_mod,
    w_qkv,
    text_ids,
    text_length,
    text_table,
    text_mod,
    w_text,
    w_out,
    out_bias,
):
    frame_count, row_count, col_count, chan_count = features.shape
    width_full = patch_weight.shape[1]
    values = features.astype(jnp.float32)
    grouped = values.reshape(frame_count, row_count, col_count, GN_GROUPS, chan_count // GN_GROUPS)
    group_sums = jnp.sum(grouped, axis=(0, 1, 2, 4))
    group_squares = jnp.sum(grouped * grouped, axis=(0, 1, 2, 4))
    group_sums, group_squares = lax.psum((group_sums, group_squares), ("seq", "head"))
    cell_count = (
        frame_count
        * row_count
        * col_count
        * (chan_count // GN_GROUPS)
        * lax.axis_size("seq")
        * lax.axis_size("head")
    )
    group_mean = group_sums / cell_count
    group_scale = lax.rsqrt(group_squares / cell_count - group_mean * group_mean + eps_norm)
    normed = ((grouped - group_mean[:, None]) * group_scale[:, None]).reshape(
        frame_count, row_count, col_count, chan_count
    )
    activated = jax.nn.silu(normed * gn_gain + gn_bias).astype(jnp.bfloat16)
    rimmed = with_halo(activated, (("seq", 1), ("head", 2)), 1)
    padded = jnp.concatenate([rimmed[:1], rimmed[:1], rimmed], axis=0)
    windows = []
    for time_off in range(3):
        for row_off in range(3):
            for col_off in range(3):
                windows.append(
                    padded[
                        time_off : time_off + frame_count,
                        row_off : row_off + row_count,
                        col_off : col_off + col_count,
                    ]
                )
    stacked = jnp.stack(windows, axis=3)
    latent_chans = conv_weight.shape[3]
    kernels = conv_weight.reshape(27, latent_chans, chan_count)
    latent_sum = jnp.einsum("fyxkc,kzc->fyxz", stacked, kernels, preferred_element_type=jnp.float32)
    latent = (latent_sum + conv_bias).astype(jnp.bfloat16)
    patches = patchify(latent)
    hidden, own_modulated = embed_tokens(patches, patch_weight, patch_bias, image_mod)
    modulated = lax.all_gather(own_modulated, "head", axis=0, tiled=True)
    token_count = modulated.shape[0]
    head_width = w_qkv.shape[2]
    heads_here = head_width // HD
    qkv = jnp.einsum(
        "nd,dkj->nkj",
        modulated,
        lax.all_gather(w_qkv, "seq", axis=0, tiled=True),
        preferred_element_type=jnp.float32,
    ).astype(jnp.bfloat16)
    context = jnp.take(text_table, text_ids, axis=1).astype(jnp.float32)
    text_weight = w_text.astype(jnp.float32)
    text_gain = 1.0 + text_mod[1]
    text_shift = text_mod[0]
    text_sums, text_squares = lax.psum(
        (jnp.sum(context, axis=0), jnp.sum(context * context, axis=0)), "seq"
    )
    text_mean = text_sums / width_full
    text_scale = lax.rsqrt(text_squares / width_full - text_mean * text_mean + eps_norm)
    text_normed = (context - text_mean) * text_scale * text_gain[:, None] + text_shift[:, None]
    partial_kv = jnp.einsum(
        "dt,dkj->tkj", text_normed, text_weight, precision=lax.Precision.HIGHEST
    )
    text_kv = lax.psum(partial_kv, "seq")
    text_kv = text_kv.astype(jnp.bfloat16)
    text_count = text_kv.shape[0]
    text_valid = jnp.arange(text_count, dtype=jnp.int32) < text_length[0]
    query = qkv[:, 0].reshape(token_count, heads_here, HD)
    text_keys = text_kv[:, 0].reshape(text_count, heads_here, HD)
    text_values = text_kv[:, 1].reshape(text_count, heads_here, HD)
    first_state = text_start(query, text_keys, text_values, text_valid)
    image_kv = qkv[:, 1:3]
    run_top, run_total, run_acc = attend_rows(
        query, first_state, lax.all_gather(image_kv, "seq", axis=0, tiled=True)
    )
    attended = (
        (run_acc / run_total[..., None]).astype(jnp.bfloat16).reshape(token_count, head_width)
    )
    projected = (
        lax.psum_scatter(
            jnp.dot(attended, w_out, preferred_element_type=jnp.float32),
            "head",
            scatter_dimension=0,
            tiled=True,
        )
        + out_bias
    )
    block_out = (hidden + image_mod[2] * projected).astype(jnp.bfloat16)
    return block_out.reshape(frame_count, row_count // 2, col_count // 2, width_full)


def solution(mesh):
    return jax.shard_map(
        body,
        mesh=mesh,
        in_specs=(
            P(None, "seq", "head", None),
            P(),
            P(),
            P(),
            P(),
            P(),
            P(),
            P(),
            P("seq", None, "head"),
            P(),
            P(),
            P("seq", None),
            P(None, "seq"),
            P("seq", None, "head"),
            P("head", None),
            P(),
        ),
        out_specs=P(None, "seq", "head", None),
        check_vma=False,
    )
```

profile of v0, /device:TPU:0, one launch (start us, length us, event | category | flops | bytes accessed | tf_op | source)
XLA Modules:
  0.0 285.2 jit_solution(11076966553390359524)
XLA Ops:
  6.5 0.7 all-gather.3.cloned.1.call-update
  7.3 0.9 convert_reduce_fusion.1
  8.6 43.1 %all-reduce = (f32[32]{0:T(128)S(1)}, f32[32]{0:T(128)S(1)}) all-reduce(f32[32]{0:T(128)S(1)} %reduce_sum.92, f32[32]{0:T(128)S(1)} %reduce_sum.89), channel_id=1, replica_groups=mesh['seq'=16,'head'=2] {'seq','head'}, use_global_device_ids=true, to_apply=%region_5.6 | all-reduce | flops 64 | bytes 512 | tf_op jit(solution)/shard_map/psum | solution.py:108
  52.0 1.0 fusion.41
  52.9 1.8 collective-permute-start
  54.7 1.3 collective-permute-start.1
  56.7 1.0 fusion.78
  57.7 0.7 compare_and_fusion
  58.4 1.5 collective-permute-done.1
  59.9 2.5 collective-permute-start.2
  62.4 1.3 collective-permute-start.3
  63.7 10.1 %copy.82 = bf16[192,16384]{0,1:T(8,128)(2,1)} copy(bf16[192,16384]{1,0:T(8,128)(2,1)} %param.27) | data formatting | bytes 12582912 | tf_op args[11]
  73.8 6.2 %gather_fusion = bf16[512,192]{1,0:T(8,128)(2,1)S(1)} fusion(bf16[192,16384]{0,1:T(8,128)(2,1)} %copy.82, s32[1024]{0:T(1024)S(1)} %pad_clamp_fusion), kind=kCustom, calls=%fused_computation | custom fusion | bytes 395264 | tf_op jit(solution)/shard_map/jit(_take)/gather | solution.py:153
  82.9 5.9 %all_gather.9 = bf16[32,3072]{1,0:T(8,128)(2,1)S(1)} all-gather(bf16[16,3072]{1,0:T(8,128)(2,1)S(1)} %add_convert_fusion.1), channel_id=1, replica_groups=mesh['seq'=16,'head'=2] {'head'}, dimensions={0}, use_global_device_ids=true | all-gather | bytes 294912 | tf_op jit(solution)/shard_map/all_gather | solution.py:143
  88.8 23.2 %all-gather.3.cloned.1.call-done = bf16[3072,3,1024]{2,0,1:T(8,128)(2,1)} async-done(((bf16[192,3,1024]{2,0,1:T(8,128)(2,1)}), bf16[3072,3,1024]{2,0,1:T(8,128)(2,1)}) %all-gather.3.cloned.1.call-update) | async-done | bytes 18874384 | tf_op jit(solution)/shard_map/all_gather | solution.py:150
  112.0 9.7 %convolution_convert_fusion = bf16[32,3,1024]{2,0,1:T(8,128)(2,1)S(1)} fusion(bf16[3072,3,1024]{2,0,1:T(8,128)(2,1)} %all-gather.3.cloned.1.call-done, bf16[32,3072]{1,0:T(8,128)(2,1)S(1)} %all_gather.9), kind=kOutput, calls=%fused_computation.7 | convolution fusion | flops 604078080 | bytes 19267584 | tf_op jit(solution)/shard_map/nd,dkj->nkj/dot_general | solution.py:147
  122.8 33.0 %all-reduce.1 = (f32[512]{0:T(512)S(1)}, f32[512]{0:T(512)S(1)}) all-reduce(f32[512]{0:T(512)S(1)} %get-tuple-element.16, f32[512]{0:T(512)S(1)} %get-tuple-element.15), channel_id=1, replica_groups=mesh['seq'=16,'head'=2] {'seq'}, use_global_device_ids=true, to_apply=%region_9.10 | all-reduce | flops 1024 | bytes 8192 | tf_op jit(solution)/shard_map/psum | solution.py:157
  155.8 3.9 %fusion.12 = f32[512,2,1024]{2,0,1:T(8,128)} fusion(bf16[192,2,1024]{2,1,0:T(2,128)(2,1)S(1)} %copy-done, f32[192]{0:T(256)S(1)} %bitcast.263, f32[192]{0:T(256)S(1)} %bitcast.262, f32[512]{0:T(512)S(1)} %get-tuple-element.47, f32[512]{0:T(512)S(1)} %get-tuple-element.46, bf16[512,192]{1,0:T(8,128)(2,1)S(1)} %gather_fusion, ...), kind=kOutput, calls=%fused_computation.24 | convolution fusion | flops 2416508928 | bytes 5183488 | tf_op jit(solution)/shard_map/dt,dkj->tkj/dot_general | solution.py:163
  159.7 94.6 %all-reduce.3 = bf16[512,2,1024]{2,0,1:T(8,128)(2,1)S(1)} all-reduce(f32[512,2,1024]{2,0,1:T(8,128)} %fusion.12), channel_id=1, replica_groups=mesh['seq'=16,'head'=2] {'seq'}, use_global_device_ids=true, to_apply=%region_10.11 | all-reduce | flops 1048576 | bytes 6291456 | tf_op jit(solution)/shard_map/psum | solution.py:166
  255.8 1.3 fusion.80
  257.0 2.4 copy.103
  261.9 1.9 fusion.43
  263.9 13.2 %reduce-scatter.2.cloned.1.call-done = f32[16,3072]{1,0:T(8,128)} async-done(((f32[32,3072]{1,0:T(8,128)}), f32[16,3072]{1,0:T(8,128)}) %reduce-scatter.2.cloned.1.call-update) | async-done | bytes 196624 | tf_op jit(solution)/shard_map/reduce_scatter | solution.py:182
  277.1 1.0 add_convert_fusion
  (106 shorter events, 9.0 us)
Async XLA Ops:
  6.5 149.3 %copy-start = (bf16[192,2,1024]{2,1,0:T(2,128)(2,1)S(1)}, bf16[192,2,1024]{2,1,0:T(2,128)(2,1)}, u32[]{:S(2)}) copy-start(bf16[192,2,1024]{2,1,0:T(2,128)(2,1)} %param.29) | copy-start | bytes 2359300
  6.5 105.4 %all-gather.3.cloned.1.call-start = ((), (), s32[]{:S(2)}) async-start(), calls=%async_computation.1 | async-start | bytes 20054016 | tf_op jit(solution)/shard_map/all_gather | solution.py:150
  7.3 249.8 %all-gather.5.cloned.1.call-start = ((), (), s32[]{:S(2)}) async-start(), calls=%async_computation.2 | async-start | bytes 2228224 | tf_op jit(solution)/shard_map/all_gather | solution.py:176
  52.9 5.4 %collective-permute-start = (bf16[8,1,4,512]{3,0,2,1:T(8,128)(2,1)S(1)}, bf16[8,1,4,512]{3,0,2,1:T(8,128)(2,1)S(1)}, u32[]{:S(2)}, u32[]{:S(2)}) collective-permute-start(bf16[8,1,4,512]{3,0,2,1:T(8,128)(2,1)S(1)} %get-tuple-element.41), channel_id=1, source_target_pairs={{0,2},{2,4},{4,6},{6,8},{8,10},{10,12},{12,14},{14,16},{16,18},{18... | collective-permute-start | bytes 98312 | tf_op jit(solution)/shard_map/ppermute | solution.py:20
  54.7 5.2 %collective-permute-start.1 = (bf16[8,1,4,512]{3,0,2,1:T(8,128)(2,1)S(1)}, bf16[8,1,4,512]{3,0,2,1:T(8,128)(2,1)S(1)}, u32[]{:S(2)}, u32[]{:S(2)}) collective-permute-start(bf16[8,1,4,512]{3,0,2,1:T(8,128)(2,1)S(1)} %get-tuple-element.42), channel_id=1, source_target_pairs={{2,0},{4,2},{6,4},{8,6},{10,8},{12,10},{14,12},{16,14},{18,16},{20... | collective-permute-start | bytes 98312 | tf_op jit(solution)/shard_map/ppermute | solution.py:22
  59.9 20.1 %collective-permute-start.2 = (bf16[8,4,1,512]{3,0,2,1:T(8,128)(2,1)S(1)}, bf16[8,4,1,512]{3,0,2,1:T(8,128)(2,1)S(1)}, u32[]{:S(2)}, u32[]{:S(2)}) collective-permute-start(bf16[8,4,1,512]{3,0,2,1:T(8,128)(2,1)S(1)} %get-tuple-element.39), channel_id=1, source_target_pairs={{0,1},{2,3},{4,5},{6,7},{8,9},{10,11},{12,13},{14,15},{16,17},{18,... | collective-permute-start | bytes 98312 | tf_op jit(solution)/shard_map/ppermute | solution.py:20
  62.4 17.6 %collective-permute-start.3 = (bf16[8,4,1,512]{3,0,2,1:T(8,128)(2,1)S(1)}, bf16[8,4,1,512]{3,0,2,1:T(8,128)(2,1)S(1)}, u32[]{:S(2)}, u32[]{:S(2)}) collective-permute-start(bf16[8,4,1,512]{3,0,2,1:T(8,128)(2,1)S(1)} %get-tuple-element.40), channel_id=1, source_target_pairs={{1,0},{3,2},{5,4},{7,6},{9,8},{11,10},{13,12},{15,14},{17,16},{19,... | collective-permute-start | bytes 98312 | tf_op jit(solution)/shard_map/ppermute | solution.py:22
  80.3 0.8 copy-start.1
  80.4 0.8 copy-start.7
  80.4 0.8 copy-start.8
  80.5 1.0 copy-start.3
  80.5 1.0 copy-start.9
  80.8 1.5 copy-start.4
  80.8 1.5 copy-start.5
  88.8 67.0 %copy-start.10 = (f32[2,192]{1,0:T(2,128)S(1)}, f32[2,192]{1,0:T(2,128)}, u32[]{:S(2)}) copy-start(f32[2,192]{1,0:T(2,128)} %param.28) | copy-start | bytes 4612
  122.4 154.7 %reduce-scatter.2.cloned.1.call-start = ((), (), s32[]{:S(2)}) async-start(), calls=%async_computation.3 | async-start | bytes 589824 | tf_op jit(solution)/shard_map/reduce_scatter | solution.py:182
  257.0 4.9 %slice-start = ((s8[6291456]{0:T(1024)(128)(4,1)}), s8[4194304]{0:T(1024)(128)(4,1)S(1)}, s32[]{:S(2)}) async-start(s8[6291456]{0:T(1024)(128)(4,1)} %bitcast.249), calls=%async_computation.4 | async-start | bytes 8388608
  259.4 2.5 slice-start.1
  259.6 1.2 copy-start.2
  261.9 15.2 %copy-start.6 = (f32[3072]{0:T(1024)S(1)}, f32[3072]{0:T(1024)}, u32[]{:S(2)}) copy-start(f32[3072]{0:T(1024)} %param.31) | copy-start | bytes 36868
Sparse Core Ops, SparseCore 0:
  8.9 103.0 all-gather.2
  122.5 42.3 all-gather.4
  264.0 12.9 reduce-scatter.1
where the time goes:
time: 286 us; the launch traced here: 285 us
  blocking collectives  177 us (62%)
  waiting for transfers between devices  38.6 us (13%)
  local copies, waits for them, and re-layouts  22.7 us (8%)
  matrix products  19.1 us (7%)
  between operations  14.3 us (5%)
  starting transfers between devices  6.94 us (2%)
  other arithmetic  6.94 us (2%)
    psum x1, blocking collectives, body(): text_kv = lax.psum(partial_kv, 'seq')  94.6 us
    psum x1, blocking collectives, body(): lax.psum((group_sums, group_squares), ('seq', 'head'))  43.1 us
    psum x1, blocking collectives, body(): lax.psum((jnp.sum(context, axis=0), jnp.sum(context * context, axis=0)),...  33 us
    all_gather x1, waiting for transfers between devices, body(): lax.all_gather(w_qkv, 'seq', axis=0, tiled=True)  23.2 us
    unnamed x56, local copies, waits for them, and re-layouts  14.5 us
    reduce_scatter x1, waiting for transfers between devices, body(): lax.psum_scatter(jnp.dot(attended, w_out, preferred_element_type=jnp.floa...  13.2 us
    dot_general x1, matrix products, body(): jnp.einsum('nd,dkj->nkj', modulated, lax.all_gather(w_qkv, 'seq', axis=0,...  9.7 us
    gather x1, local copies, waits for them, and re-layouts, body(): context = jnp.take(text_table, text_ids, axis=1).astype(jnp.float32)  6.18 us
  transfers between devices with their start and end apart: 7, of which 3 were waited for; matrix products, arithmetic and copies ran while one was open for 10% of the time, Pallas kernels for 0%

commit v1 on v0

--- a/solution.py
+++ b/solution.py
@@ -7,6 +7,27 @@
 HD = 128
 GN_GROUPS = 32
 eps_norm = 1e-06
+
+
+def gather_around(array, axis, dim):
+    size, index, rows = (lax.axis_size(axis), lax.axis_index(axis), array.shape[dim])
+    ahead = [(i, (i + 1) % size) for i in range(size)]
+    left = [(i, (i - 1) % size) for i in range(size)]
+    whole = jnp.zeros((*array.shape[:dim], size * rows, *array.shape[dim + 1 :]), array.dtype)
+    whole = lax.dynamic_update_slice_in_dim(whole, array, index * rows, axis=dim)
+    from_left = from_right = array
+    halfway = size // 2
+    for hop in range(1, halfway + 1):
+        from_left = lax.ppermute(from_left, axis, ahead)
+        whole = lax.dynamic_update_slice_in_dim(
+            whole, from_left, (index - hop) % size * rows, axis=dim
+        )
+        if hop < size - halfway:
+            from_right = lax.ppermute(from_right, axis, left)
+            whole = lax.dynamic_update_slice_in_dim(
+                whole, from_right, (index + hop) % size * rows, axis=dim
+            )
+    return whole
 
 
 def with_halo(cells, sides, width):
@@ -145,10 +166,7 @@
     head_width = w_qkv.shape[2]
     heads_here = head_width // HD
     qkv = jnp.einsum(
-        "nd,dkj->nkj",
-        modulated,
-        lax.all_gather(w_qkv, "seq", axis=0, tiled=True),
-        preferred_element_type=jnp.float32,
+        "nd,dkj->nkj", modulated, gather_around(w_qkv, "seq", 0), preferred_element_type=jnp.float32
     ).astype(jnp.bfloat16)
     context = jnp.take(text_table, text_ids, axis=1).astype(jnp.float32)
     text_weight = w_text.astype(jnp.float32)

time: 286 us -> 470 us (1.64)
  starting transfers between devices: 6.94 us -> 139 us
  local copies, waits for them, and re-layouts: 22.7 us -> 54.6 us
  blocking collectives: 177 us -> 191 us
    ppermute x0 -> x15, starting transfers between devices: none -> 130 us  [the longest x8 122 us: gather_around(): from_left = lax.ppermute(from_left, axis, ahead)]
    ppermute x0 -> x15, waiting for transfers between devices: none -> 25.8 us  [the longest x8 25.8 us: gather_around(): from_left = lax.ppermute(from_left, axis, ahead)]
    dynamic_update_slice x0 -> x16, local copies, waits for them, and re-layouts: none -> 24.3 us  [the longest x7 11.7 us: gather_around(): lax.dynamic_update_slice_in_dim(whole, from_right, (index + hop) % size *...]
    all_gather x1 -> x0, waiting for transfers between devices: 23.2 us -> none  [body(): lax.all_gather(w_qkv, 'seq', axis=0, tiled=True)]
    psum x1, blocking collectives: 43.1 us -> 58.4 us  [body(): lax.psum((group_sums, group_squares), ('seq', 'head'))]
    broadcast_in_dim x0 -> x1, local copies, waits for them, and re-layouts: none -> 6.69 us  [gather_around(): jnp.zeros((*array.shape[:dim], size * rows, *array.shape[dim + 1:]), arra...]
    unnamed x56 -> x96, local copies, waits for them, and re-layouts: 14.5 us -> 15.5 us
  transfers between devices with their start and end apart: 7 -> 21, of which waited for: 3 -> 6; matrix products, arithmetic and copies ran while one was open for 10% -> 13% of each run, Pallas kernels for 0% -> 0%
where the time goes in v1:
time: 470 us; the launch traced here: 469 us
  blocking collectives  191 us (41%)
  starting transfers between devices  139 us (30%)
  local copies, waits for them, and re-layouts  54.6 us (12%)
  waiting for transfers between devices  40.4 us (9%)
  matrix products  20.2 us (4%)
  between operations  15.1 us (3%)
  other arithmetic  8.83 us (2%)
    ppermute x8, starting transfers between devices, gather_around(): from_left = lax.ppermute(from_left, axis, ahead)  122 us
    psum x1, blocking collectives, body(): text_kv = lax.psum(partial_kv, 'seq')  94.4 us
    psum x1, blocking collectives, body(): lax.psum((group_sums, group_squares), ('seq', 'head'))  58.4 us
    psum x1, blocking collectives, body(): lax.psum((jnp.sum(context, axis=0), jnp.sum(context * context, axis=0)),...  32.2 us
    ppermute x8, waiting for transfers between devices, gather_around(): from_left = lax.ppermute(from_left, axis, ahead)  25.8 us
    unnamed x96, local copies, waits for them, and re-layouts  15.5 us
    reduce_scatter x1, waiting for transfers between devices, body(): lax.psum_scatter(jnp.dot(attended, w_out, preferred_element_type=jnp.floa...  14.5 us
    dynamic_update_slice x7, local copies, waits for them, and re-layouts, gather_around(): lax.dynamic_update_slice_in_dim(whole, from_right, (index + hop) % size *...  11.7 us
  transfers between devices with their start and end apart: 21, of which 6 were waited for; matrix products, arithmetic and copies ran while one was open for 13% of the time, Pallas kernels for 0%

profile of v1, /device:TPU:0, one launch (start us, length us, event | category | flops | bytes accessed | tf_op | source)
XLA Modules:
  0.0 468.7 jit_solution(11956633674230045455)
XLA Ops:
  8.3 5.1 %collective-permute-start.5 = (bf16[192,3,1024]{2,0,1:T(8,128)(2,1)}, bf16[192,3,1024]{2,0,1:T(8,128)(2,1)}, u32[]{:S(2)}, u32[]{:S(2)}) collective-permute-start(bf16[192,3,1024]{2,0,1:T(8,128)(2,1)} %param.24), channel_id=1, source_target_pairs={{0,30},{2,0},{4,2},{6,4},{8,6},{10,8},{12,10},{14,12},{16,14},{18,... | collective-permute-start | bytes 3538952 | tf_op jit(solution)/shard_map/ppermute | solution.py:26
  13.4 58.4 %all-reduce = (f32[32]{0:T(128)S(1)}, f32[32]{0:T(128)S(1)}) all-reduce(f32[32]{0:T(128)S(1)} %reduce_sum.92, f32[32]{0:T(128)S(1)} %reduce_sum.89), channel_id=1, replica_groups=mesh['seq'=16,'head'=2] {'seq','head'}, use_global_device_ids=true, to_apply=%region_5.6 | all-reduce | flops 64 | bytes 512 | tf_op jit(solution)/shard_map/psum | solution.py:129
  79.2 6.7 %broadcast_in_dim.49 = bf16[3072,3,1024]{2,0,1:T(8,128)(2,1)} broadcast(bf16[]{:T(256)} %constant.145.clone.1), dimensions={} | broadcast | bytes 18874370 | tf_op jit(solution)/shard_map/broadcast_in_dim | solution.py:16
  87.0 4.2 collective-permute-start.2
  92.8 10.1 %copy.82 = bf16[192,16384]{0,1:T(8,128)(2,1)} copy(bf16[192,16384]{1,0:T(8,128)(2,1)} %param.27) | data formatting | bytes 12582912 | tf_op args[11]
  102.8 6.0 %gather_fusion = bf16[512,192]{1,0:T(8,128)(2,1)S(1)} fusion(bf16[192,16384]{0,1:T(8,128)(2,1)} %copy.82, s32[1024]{0:T(1024)S(1)} %pad_clamp_fusion), kind=kCustom, calls=%fused_computation | custom fusion | bytes 395264 | tf_op jit(solution)/shard_map/jit(_take)/gather | solution.py:171
  111.3 3.0 collective-permute-start.7
  114.2 13.8 %collective-permute-done.6 = bf16[192,3,1024]{2,0,1:T(8,128)(2,1)S(1)} collective-permute-done((bf16[192,3,1024]{2,0,1:T(8,128)(2,1)S(1)}, bf16[192,3,1024]{2,0,1:T(8,128)(2,1)S(1)}, u32[]{:S(2)}, u32[]{:S(2)}) %collective-permute-start.6) | collective-permute-done | bytes 1179680 | tf_op jit(solution)/shard_map/ppermute | solution.py:21
  128.0 10.9 %collective-permute-start.8 = (bf16[192,3,1024]{2,0,1:T(8,128)(2,1)S(1)}, bf16[192,3,1024]{2,0,1:T(8,128)(2,1)S(1)}, u32[]{:S(2)}, u32[]{:S(2)}) collective-permute-start(bf16[192,3,1024]{2,0,1:T(8,128)(2,1)S(1)} %collective-permute-done.6), channel_id=1, source_target_pairs={{0,2},{2,4},{4,6},{6,8},{8,10},{10,12},{12,14},{14,16},{16,18},{18... | collective-permute-start | bytes 3538952 | tf_op jit(solution)/shard_map/ppermute | solution.py:21
  140.0 6.5 %collective-permute-done.8 = bf16[192,3,1024]{2,0,1:T(8,128)(2,1)S(1)} collective-permute-done((bf16[192,3,1024]{2,0,1:T(8,128)(2,1)S(1)}, bf16[192,3,1024]{2,0,1:T(8,128)(2,1)S(1)}, u32[]{:S(2)}, u32[]{:S(2)}) %collective-permute-start.8) | collective-permute-done | bytes 1179680 | tf_op jit(solution)/shard_map/ppermute | solution.py:21
  146.5 20.0 %collective-permute-start.10 = (bf16[192,3,1024]{2,0,1:T(8,128)(2,1)S(1)}, bf16[192,3,1024]{2,0,1:T(8,128)(2,1)S(1)}, u32[]{:S(2)}, u32[]{:S(2)}) collective-permute-start(bf16[192,3,1024]{2,0,1:T(8,128)(2,1)S(1)} %collective-permute-done.8), channel_id=1, source_target_pairs={{0,2},{2,4},{4,6},{6,8},{8,10},{10,12},{12,14},{14,16},{16,18},{18... | collective-permute-start | bytes 3538952 | tf_op jit(solution)/shard_map/ppermute | solution.py:21
  166.7 2.8 collective-permute-done.10
  169.4 23.8 %collective-permute-start.12 = (bf16[192,3,1024]{2,0,1:T(8,128)(2,1)S(1)}, bf16[192,3,1024]{2,0,1:T(8,128)(2,1)}, u32[]{:S(2)}, u32[]{:S(2)}) collective-permute-start(bf16[192,3,1024]{2,0,1:T(8,128)(2,1)S(1)} %collective-permute-done.10), channel_id=1, source_target_pairs={{0,2},{2,4},{4,6},{6,8},{8,10},{10,12},{12,14},{14,16},{16,18},{18... | collective-permute-start | bytes 3538952 | tf_op jit(solution)/shard_map/ppermute | solution.py:21
  195.9 25.1 %collective-permute-start.14 = (bf16[192,3,1024]{2,0,1:T(8,128)(2,1)}, bf16[192,3,1024]{2,0,1:T(8,128)(2,1)}, u32[]{:S(2)}, u32[]{:S(2)}) collective-permute-start(bf16[192,3,1024]{2,0,1:T(8,128)(2,1)} %collective-permute-done.12), channel_id=1, source_target_pairs={{0,2},{2,4},{4,6},{6,8},{8,10},{10,12},{12,14},{14,16},{16,18},{18... | collective-permute-start | bytes 3538952 | tf_op jit(solution)/shard_map/ppermute | solution.py:21
  223.7 25.9 %collective-permute-start.16 = (bf16[192,3,1024]{2,0,1:T(8,128)(2,1)}, bf16[192,3,1024]{2,0,1:T(8,128)(2,1)S(1)}, u32[]{:S(2)}, u32[]{:S(2)}) collective-permute-start(bf16[192,3,1024]{2,0,1:T(8,128)(2,1)} %collective-permute-done.14), channel_id=1, source_target_pairs={{0,2},{2,4},{4,6},{6,8},{8,10},{10,12},{12,14},{14,16},{16,18},{18... | collective-permute-start | bytes 3538952 | tf_op jit(solution)/shard_map/ppermute | solution.py:21
  249.7 5.9 %all_gather.6 = bf16[32,3072]{1,0:T(8,128)(2,1)S(1)} all-gather(bf16[16,3072]{1,0:T(8,128)(2,1)S(1)} %add_convert_fusion.1), channel_id=1, replica_groups=mesh['seq'=16,'head'=2] {'head'}, dimensions={0}, use_global_device_ids=true | all-gather | bytes 294912 | tf_op jit(solution)/shard_map/all_gather | solution.py:164
  256.7 2.5 constant_dynamic-update-slice_fusion.13
  263.7 14.5 %collective-permute-start.18 = (bf16[192,3,1024]{2,0,1:T(8,128)(2,1)S(1)}, bf16[192,3,1024]{2,0,1:T(8,128)(2,1)S(1)}, u32[]{:S(2)}, u32[]{:S(2)}) collective-permute-start(bf16[192,3,1024]{2,0,1:T(8,128)(2,1)S(1)} %collective-permute-done.16), channel_id=1, source_target_pairs={{0,2},{2,4},{4,6},{6,8},{8,10},{10,12},{12,14},{14,16},{16,18},{18... | collective-permute-start | bytes 3538952 | tf_op jit(solution)/shard_map/ppermute | solution.py:21
  287.6 2.4 constant_dynamic-update-slice_fusion.4
  294.4 9.7 %convolution_convert_fusion = bf16[32,3,1024]{2,0,1:T(8,128)(2,1)S(1)} fusion(bf16[3072,3,1024]{2,0,1:T(8,128)(2,1)} %constant_dynamic-update-slice_fusion, bf16[32,3072]{1,0:T(8,128)(2,1)S(1)} %all_gather.6), kind=kOutput, calls=%fused_computation.7 | convolution fusion | flops 604078080 | bytes 19267584 | tf_op jit(solution)/shard_map/nd,dkj->nkj/dot_general | solution.py:168
  305.5 32.2 %all-reduce.1 = (f32[512]{0:T(512)S(1)}, f32[512]{0:T(512)S(1)}) all-reduce(f32[512]{0:T(512)S(1)} %get-tuple-element.16, f32[512]{0:T(512)S(1)} %get-tuple-element.15), channel_id=1, replica_groups=mesh['seq'=16,'head'=2] {'seq'}, use_global_device_ids=true, to_apply=%region_9.10 | all-reduce | flops 1024 | bytes 8192 | tf_op jit(solution)/shard_map/psum | solution.py:175
  337.7 3.9 fusion.12
  341.6 94.4 %all-reduce.3 = bf16[512,2,1024]{2,0,1:T(8,128)(2,1)S(1)} all-reduce(f32[512,2,1024]{2,0,1:T(8,128)} %fusion.12), channel_id=1, replica_groups=mesh['seq'=16,'head'=2] {'seq'}, use_global_device_ids=true, to_apply=%region_10.11 | all-reduce | flops 1048576 | bytes 6291456 | tf_op jit(solution)/shard_map/psum | solution.py:184
  445.7 14.5 %reduce-scatter.2.cloned.1.call-done = f32[16,3072]{1,0:T(8,128)} async-done(((f32[32,3072]{1,0:T(8,128)}), f32[16,3072]{1,0:T(8,128)}) %reduce-scatter.2.cloned.1.call-update) | async-done | bytes 196624 | tf_op jit(solution)/shard_map/reduce_scatter | solution.py:200
  (190 shorter events, 51.4 us)
Async XLA Ops:
  6.5 331.1 %copy-start = (bf16[192,2,1024]{2,1,0:T(2,128)(2,1)S(1)}, bf16[192,2,1024]{2,1,0:T(2,128)(2,1)}, u32[]{:S(2)}) copy-start(bf16[192,2,1024]{2,1,0:T(2,128)(2,1)} %param.29) | copy-start | bytes 2359300
  6.5 432.3 %all-gather.2.cloned.1.call-start = ((), (), s32[]{:S(2)}) async-start(), calls=%async_computation.1 | async-start | bytes 2228224 | tf_op jit(solution)/shard_map/all_gather | solution.py:194
  6.5 103.0 %collective-permute-start.4 = (bf16[192,3,1024]{2,0,1:T(8,128)(2,1)}, bf16[192,3,1024]{2,0,1:T(8,128)(2,1)S(1)}, u32[]{:S(2)}, u32[]{:S(2)}) collective-permute-start(bf16[192,3,1024]{2,0,1:T(8,128)(2,1)} %param.24), channel_id=1, source_target_pairs={{0,2},{2,4},{4,6},{6,8},{8,10},{10,12},{12,14},{14,16},{16,18},{18... | collective-permute-start | bytes 3538952 | tf_op jit(solution)/shard_map/ppermute | solution.py:21
  8.3 103.0 %collective-permute-start.5 = (bf16[192,3,1024]{2,0,1:T(8,128)(2,1)}, bf16[192,3,1024]{2,0,1:T(8,128)(2,1)}, u32[]{:S(2)}, u32[]{:S(2)}) collective-permute-start(bf16[192,3,1024]{2,0,1:T(8,128)(2,1)} %param.24), channel_id=1, source_target_pairs={{0,30},{2,0},{4,2},{6,4},{8,6},{10,8},{12,10},{14,12},{16,14},{18,... | collective-permute-start | bytes 3538952 | tf_op jit(solution)/shard_map/ppermute | solution.py:26
  73.1 13.9 %collective-permute-start = (bf16[8,1,4,512]{3,0,2,1:T(8,128)(2,1)S(1)}, bf16[8,1,4,512]{3,0,2,1:T(8,128)(2,1)S(1)}, u32[]{:S(2)}, u32[]{:S(2)}) collective-permute-start(bf16[8,1,4,512]{3,0,2,1:T(8,128)(2,1)S(1)} %get-tuple-element.41), channel_id=1, source_target_pairs={{0,2},{2,4},{4,6},{6,8},{8,10},{10,12},{12,14},{14,16},{16,18},{18... | collective-permute-start | bytes 98312 | tf_op jit(solution)/shard_map/ppermute | solution.py:41
  74.4 12.6 %collective-permute-start.1 = (bf16[8,1,4,512]{3,0,2,1:T(8,128)(2,1)S(1)}, bf16[8,1,4,512]{3,0,2,1:T(8,128)(2,1)S(1)}, u32[]{:S(2)}, u32[]{:S(2)}) collective-permute-start(bf16[8,1,4,512]{3,0,2,1:T(8,128)(2,1)S(1)} %get-tuple-element.42), channel_id=1, source_target_pairs={{2,0},{4,2},{6,4},{8,6},{10,8},{12,10},{14,12},{16,14},{18,16},{20... | collective-permute-start | bytes 98312 | tf_op jit(solution)/shard_map/ppermute | solution.py:43
  87.0 21.9 %collective-permute-start.2 = (bf16[8,4,1,512]{3,0,2,1:T(8,128)(2,1)S(1)}, bf16[8,4,1,512]{3,0,2,1:T(8,128)(2,1)S(1)}, u32[]{:S(2)}, u32[]{:S(2)}) collective-permute-start(bf16[8,4,1,512]{3,0,2,1:T(8,128)(2,1)S(1)} %get-tuple-element.39), channel_id=1, source_target_pairs={{0,1},{2,3},{4,5},{6,7},{8,9},{10,11},{12,13},{14,15},{16,17},{18,... | collective-permute-start | bytes 98312 | tf_op jit(solution)/shard_map/ppermute | solution.py:41
  91.2 17.7 %collective-permute-start.3 = (bf16[8,4,1,512]{3,0,2,1:T(8,128)(2,1)S(1)}, bf16[8,4,1,512]{3,0,2,1:T(8,128)(2,1)S(1)}, u32[]{:S(2)}, u32[]{:S(2)}) collective-permute-start(bf16[8,4,1,512]{3,0,2,1:T(8,128)(2,1)S(1)} %get-tuple-element.40), channel_id=1, source_target_pairs={{1,0},{3,2},{5,4},{7,6},{9,8},{11,10},{13,12},{15,14},{17,16},{19,... | collective-permute-start | bytes 98312 | tf_op jit(solution)/shard_map/ppermute | solution.py:43
  109.6 18.5 %collective-permute-start.6 = (bf16[192,3,1024]{2,0,1:T(8,128)(2,1)S(1)}, bf16[192,3,1024]{2,0,1:T(8,128)(2,1)S(1)}, u32[]{:S(2)}, u32[]{:S(2)}) collective-permute-start(bf16[192,3,1024]{2,0,1:T(8,128)(2,1)S(1)} %collective-permute-done.4), channel_id=1, source_target_pairs={{0,2},{2,4},{4,6},{6,8},{8,10},{10,12},{12,14},{14,16},{16,18},{18... | collective-permute-start | bytes 3538952 | tf_op jit(solution)/shard_map/ppermute | solution.py:21
  111.2 109.8 %copy-start.20 = (bf16[3,3,3,16,512]{4,3,2,1,0:T(8,128)(2,1)S(1)}, bf16[3,3,3,16,512]{4,3,2,1,0:T(8,128)(2,1)}, u32[]{:S(2)}) copy-start(bf16[3,3,3,16,512]{4,3,2,1,0:T(8,128)(2,1)} %param.19) | copy-start | bytes 1327108
  111.2 109.7 %copy-start.29 = (f32[16]{0:T(128)S(1)}, f32[16]{0:T(128)}, u32[]{:S(2)}) copy-start(f32[16]{0:T(128)} %param.20) | copy-start | bytes 196
  111.3 28.6 %collective-permute-start.7 = (bf16[192,3,1024]{2,0,1:T(8,128)(2,1)}, bf16[192,3,1024]{2,0,1:T(8,128)(2,1)S(1)}, u32[]{:S(2)}, u32[]{:S(2)}) collective-permute-start(bf16[192,3,1024]{2,0,1:T(8,128)(2,1)} %collective-permute-done.5), channel_id=1, source_target_pairs={{0,30},{2,0},{4,2},{6,4},{8,6},{10,8},{12,10},{14,12},{16,14},{18,... | collective-permute-start | bytes 3538952 | tf_op jit(solution)/shard_map/ppermute | solution.py:26
  128.0 18.4 %collective-permute-start.8 = (bf16[192,3,1024]{2,0,1:T(8,128)(2,1)S(1)}, bf16[192,3,1024]{2,0,1:T(8,128)(2,1)S(1)}, u32[]{:S(2)}, u32[]{:S(2)}) collective-permute-start(bf16[192,3,1024]{2,0,1:T(8,128)(2,1)S(1)} %collective-permute-done.6), channel_id=1, source_target_pairs={{0,2},{2,4},{4,6},{6,8},{8,10},{10,12},{12,14},{14,16},{16,18},{18... | collective-permute-start | bytes 3538952 | tf_op jit(solution)/shard_map/ppermute | solution.py:21
  139.9 26.7 %collective-permute-start.9 = (bf16[192,3,1024]{2,0,1:T(8,128)(2,1)S(1)}, bf16[192,3,1024]{2,0,1:T(8,128)(2,1)S(1)}, u32[]{:S(2)}, u32[]{:S(2)}) collective-permute-start(bf16[192,3,1024]{2,0,1:T(8,128)(2,1)S(1)} %collective-permute-done.7), channel_id=1, source_target_pairs={{0,30},{2,0},{4,2},{6,4},{8,6},{10,8},{12,10},{14,12},{16,14},{18,... | collective-permute-start | bytes 3538952 | tf_op jit(solution)/shard_map/ppermute | solution.py:26
  146.5 23.0 %collective-permute-start.10 = (bf16[192,3,1024]{2,0,1:T(8,128)(2,1)S(1)}, bf16[192,3,1024]{2,0,1:T(8,128)(2,1)S(1)}, u32[]{:S(2)}, u32[]{:S(2)}) collective-permute-start(bf16[192,3,1024]{2,0,1:T(8,128)(2,1)S(1)} %collective-permute-done.8), channel_id=1, source_target_pairs={{0,2},{2,4},{4,6},{6,8},{8,10},{10,12},{12,14},{14,16},{16,18},{18... | collective-permute-start | bytes 3538952 | tf_op jit(solution)/shard_map/ppermute | solution.py:21
  166.6 26.8 %collective-permute-start.11 = (bf16[192,3,1024]{2,0,1:T(8,128)(2,1)S(1)}, bf16[192,3,1024]{2,0,1:T(8,128)(2,1)}, u32[]{:S(2)}, u32[]{:S(2)}) collective-permute-start(bf16[192,3,1024]{2,0,1:T(8,128)(2,1)S(1)} %collective-permute-done.9), channel_id=1, source_target_pairs={{0,30},{2,0},{4,2},{6,4},{8,6},{10,8},{12,10},{14,12},{16,14},{18,... | collective-permute-start | bytes 3538952 | tf_op jit(solution)/shard_map/ppermute | solution.py:26
  169.4 26.4 %collective-permute-start.12 = (bf16[192,3,1024]{2,0,1:T(8,128)(2,1)S(1)}, bf16[192,3,1024]{2,0,1:T(8,128)(2,1)}, u32[]{:S(2)}, u32[]{:S(2)}) collective-permute-start(bf16[192,3,1024]{2,0,1:T(8,128)(2,1)S(1)} %collective-permute-done.10), channel_id=1, source_target_pairs={{0,2},{2,4},{4,6},{6,8},{8,10},{10,12},{12,14},{14,16},{16,18},{18... | collective-permute-start | bytes 3538952 | tf_op jit(solution)/shard_map/ppermute | solution.py:21
  193.5 29.8 %collective-permute-start.13 = (bf16[192,3,1024]{2,0,1:T(8,128)(2,1)}, bf16[192,3,1024]{2,0,1:T(8,128)(2,1)}, u32[]{:S(2)}, u32[]{:S(2)}) collective-permute-start(bf16[192,3,1024]{2,0,1:T(8,128)(2,1)} %collective-permute-done.11), channel_id=1, source_target_pairs={{0,30},{2,0},{4,2},{6,4},{8,6},{10,8},{12,10},{14,12},{16,14},{18,... | collective-permute-start | bytes 3538952 | tf_op jit(solution)/shard_map/ppermute | solution.py:26
  195.9 27.9 %collective-permute-start.14 = (bf16[192,3,1024]{2,0,1:T(8,128)(2,1)}, bf16[192,3,1024]{2,0,1:T(8,128)(2,1)}, u32[]{:S(2)}, u32[]{:S(2)}) collective-permute-start(bf16[192,3,1024]{2,0,1:T(8,128)(2,1)} %collective-permute-done.12), channel_id=1, source_target_pairs={{0,2},{2,4},{4,6},{6,8},{8,10},{10,12},{12,14},{14,16},{16,18},{18... | collective-permute-start | bytes 3538952 | tf_op jit(solution)/shard_map/ppermute | solution.py:21
  223.2 38.8 %collective-permute-start.15 = (bf16[192,3,1024]{2,0,1:T(8,128)(2,1)}, bf16[192,3,1024]{2,0,1:T(8,128)(2,1)S(1)}, u32[]{:S(2)}, u32[]{:S(2)}) collective-permute-start(bf16[192,3,1024]{2,0,1:T(8,128)(2,1)} %collective-permute-done.13), channel_id=1, source_target_pairs={{0,30},{2,0},{4,2},{6,4},{8,6},{10,8},{12,10},{14,12},{16,14},{18,... | collective-permute-start | bytes 3538952 | tf_op jit(solution)/shard_map/ppermute | solution.py:26
  223.7 40.0 %collective-permute-start.16 = (bf16[192,3,1024]{2,0,1:T(8,128)(2,1)}, bf16[192,3,1024]{2,0,1:T(8,128)(2,1)S(1)}, u32[]{:S(2)}, u32[]{:S(2)}) collective-permute-start(bf16[192,3,1024]{2,0,1:T(8,128)(2,1)} %collective-permute-done.14), channel_id=1, source_target_pairs={{0,2},{2,4},{4,6},{6,8},{8,10},{10,12},{12,14},{14,16},{16,18},{18... | collective-permute-start | bytes 3538952 | tf_op jit(solution)/shard_map/ppermute | solution.py:21
  262.0 30.2 %collective-permute-start.17 = (bf16[192,3,1024]{2,0,1:T(8,128)(2,1)S(1)}, bf16[192,3,1024]{2,0,1:T(8,128)(2,1)S(1)}, u32[]{:S(2)}, u32[]{:S(2)}) collective-permute-start(bf16[192,3,1024]{2,0,1:T(8,128)(2,1)S(1)} %collective-permute-done.15), channel_id=1, source_target_pairs={{0,30},{2,0},{4,2},{6,4},{8,6},{10,8},{12,10},{14,12},{16,14},{18,... | collective-permute-start | bytes 3538952 | tf_op jit(solution)/shard_map/ppermute | solution.py:26
  263.7 29.6 %collective-permute-start.18 = (bf16[192,3,1024]{2,0,1:T(8,128)(2,1)S(1)}, bf16[192,3,1024]{2,0,1:T(8,128)(2,1)S(1)}, u32[]{:S(2)}, u32[]{:S(2)}) collective-permute-start(bf16[192,3,1024]{2,0,1:T(8,128)(2,1)S(1)} %collective-permute-done.16), channel_id=1, source_target_pairs={{0,2},{2,4},{4,6},{6,8},{8,10},{10,12},{12,14},{14,16},{16,18},{18... | collective-permute-start | bytes 3538952 | tf_op jit(solution)/shard_map/ppermute | solution.py:21
  304.9 155.3 %reduce-scatter.2.cloned.1.call-start = ((), (), s32[]{:S(2)}) async-start(), calls=%async_computation.2 | async-start | bytes 589824 | tf_op jit(solution)/shard_map/reduce_scatter | solution.py:200
  (30 other events, 1118.5 us)
Sparse Core Ops, SparseCore 0:
  305.0 44.9 all-gather.1
  445.8 14.3 reduce-scatter.1
